TPU v7x, 512 devices: a whole 4x4x16 slice. The times are simulated.
512 devices in a mesh: sx: 32 (over z_hi, y, core), sy: 16 (over x, z_lo).
Axes of the slice: x: 4, y: 4, z: 16 (z_hi: 4, z_lo: 4; z = z_hi * 4 + z_lo), core: 2. Of those that a mesh axis runs over, the one named last changes fastest.
Arguments:
- forward_prop: bfloat16 [2, 2, 12, 12, 64, 4096], P(None, None, None, None, 'sx', 'sy'), may hold values from -0.08984375 to 0.08984375
- backward_prop: bfloat16 [2, 2, 12, 12, 64, 4096], P(None, None, None, None, 'sx', 'sy'), may hold values from -0.08984375 to 0.08984375
- gamma_table: int32 [16, 4, 2], replicated, may hold values from 0 to 3, as said below
- source_site: int32 [3], replicated, may hold values from 0 to 63
- momenta: int32 [32, 3], replicated, may hold values from -8 to 7
Outputs:
- corr: float32 [16, 2, 2, 64, 4096], P(None, None, None, 'sx', 'sy')
- listed: float32 [2, 16, 2, 32], replicated
Inputs may be any that keep to these rules, and one draw needn't show every extreme that they name: For every insertion g, gamma_table[g, 0..3, 0] is a permutation of 0..3; gamma_table[g, s, 1] is the power of i of that entry.
All inputs are finite; a program needn't handle non-finite values.
Results may differ from a plain program's by a relative error of at most 0.0003.
Values sent between devices are 32-bit elements; how exact they have to be, the bound alone decides.
A program may use at most 64 MiB of HBM per device.

v0:
```python
import math
import jax
import jax.numpy as jnp
from jax import lax
from jax.sharding import PartitionSpec as P

L = 64
LZ = 64
HIGHEST = lax.Precision.HIGHEST


def gamma_matrices(gamma_table):
    inserts = gamma_table.shape[0]
    columns = gamma_table[:, :, 0]
    powers = gamma_table[:, :, 1]
    spin_ids = jnp.arange(4, dtype=jnp.int32)
    matches = (columns[:, :, None] == spin_ids[None, None, :]).astype(jnp.float32)
    unit_re = (powers == 0).astype(jnp.float32) - (powers == 2).astype(jnp.float32)
    unit_im = (powers == 1).astype(jnp.float32) - (powers == 3).astype(jnp.float32)
    return (
        (matches * unit_re[:, :, None]).reshape(inserts, 16),
        (matches * unit_im[:, :, None]).reshape(inserts, 16),
    )


def dft_table(length, anchor):
    wavenum = jnp.arange(length, dtype=jnp.int32)
    offsets = jnp.mod(wavenum - anchor, length)
    phase_index = jnp.mod(offsets[:, None] * wavenum[None, :], length)
    angles = 2.0 * math.pi / length * phase_index.astype(jnp.float32)
    return (jnp.cos(angles), -jnp.sin(angles))


def complex_step(real_part, imag_part, table_re, table_im, pattern):
    out_re = jnp.einsum(pattern, real_part, table_re, precision=HIGHEST) - jnp.einsum(
        pattern, imag_part, table_im, precision=HIGHEST
    )
    out_im = jnp.einsum(pattern, real_part, table_im, precision=HIGHEST) + jnp.einsum(
        pattern, imag_part, table_re, precision=HIGHEST
    )
    return (out_re, out_im)


def transform(fields, source_site):
    table_re, table_im = dft_table(fields.shape[4], source_site[2])
    along_z = jnp.stack(
        complex_step(fields[:, 0], fields[:, 1], table_re, table_im, "nabz,zk->nabk"), 1
    )
    depth_share = along_z.shape[4] // lax.axis_size("sy")
    first_depth = lax.axis_index("sy") * depth_share
    length_y = along_z.shape[3] * lax.axis_size("sy")
    full_re, full_im = dft_table(length_y, source_site[1])
    part = lax.dynamic_slice_in_dim(
        lax.all_gather(along_z, "sy", axis=3, tiled=True), first_depth, depth_share, 4
    )
    step_re, step_im = complex_step(part[:, 0], part[:, 1], full_re, full_im, "nayc,yk->nakc")
    along_y = jnp.stack([step_re, step_im], 1)
    arrived = lax.all_to_all(along_y, "sx", split_axis=3, concat_axis=2, tiled=True)
    table_re, table_im = dft_table(arrived.shape[2], source_site[0])
    along_x = complex_step(arrived[:, 0], arrived[:, 1], table_re, table_im, "nxbc,xk->nbck")
    return jnp.stack(along_x, 1)


def apply_gammas(mat_re, mat_im, real_part, imag_part):
    extent = real_part.shape
    flat_re = real_part.reshape(extent[0], -1)
    flat_im = imag_part.reshape(extent[0], -1)
    out_re = jnp.dot(mat_re, flat_re, precision=HIGHEST) - jnp.dot(
        mat_im, flat_im, precision=HIGHEST
    )
    out_im = jnp.dot(mat_re, flat_im, precision=HIGHEST) + jnp.dot(
        mat_im, flat_re, precision=HIGHEST
    )
    return (out_re.reshape(extent), out_im.reshape(extent))


def project_sites(fields, source_site, momenta, rows_x, rows_y, length, depth):
    coord_x = lax.axis_index("sx") * rows_x + jnp.arange(rows_x, dtype=jnp.int32) - source_site[0]
    coord_y = lax.axis_index("sy") * rows_y + jnp.arange(rows_y, dtype=jnp.int32) - source_site[1]
    coord_z = jnp.arange(depth, dtype=jnp.int32) - source_site[2]
    part_x = jnp.mod(momenta[:, 0:1] * coord_x[None, :], length)
    part_y = jnp.mod(momenta[:, 1:2] * coord_y[None, :], length)
    part_z = jnp.mod(momenta[:, 2:3] * coord_z[None, :], depth)
    plane = jnp.mod(part_x[:, :, None] + part_y[:, None, :], length).astype(jnp.float32)
    angles = (
        2.0 * math.pi / length * plane[:, :, :, None]
        + 2.0 * math.pi / depth * part_z.astype(jnp.float32)[:, None, None, :]
    )
    angles = angles.reshape(momenta.shape[0], -1)
    cosine = jnp.cos(angles)
    sine = jnp.sin(angles)
    field_re = fields[:, 0].reshape(fields.shape[0], -1)
    field_im = fields[:, 1].reshape(fields.shape[0], -1)
    local_re = jnp.dot(field_re, cosine.T, precision=HIGHEST) + jnp.dot(
        field_im, sine.T, precision=HIGHEST
    )
    local_im = jnp.dot(field_im, cosine.T, precision=HIGHEST) - jnp.dot(
        field_re, sine.T, precision=HIGHEST
    )
    return (local_re, local_im)


def body(forward_prop, backward_prop, gamma_table, source_site, momenta):
    slices = forward_prop.shape[0]
    rows_x = forward_prop.shape[4]
    rows_y = backward_prop.shape[5] // LZ
    inserts = gamma_table.shape[0]
    forward = forward_prop.reshape(slices, 2, 4, 3, 12, -1)
    backward = backward_prop.reshape(slices, 2, 4, 3, 12, -1)
    pattern = "tscjn,tucjn->sutn"
    pair_re = jnp.einsum(
        pattern, backward[:, 0], forward[:, 0], preferred_element_type=jnp.float32
    ) + jnp.einsum(pattern, backward[:, 1], forward[:, 1], preferred_element_type=jnp.float32)
    pair_im = jnp.einsum(
        pattern, backward[:, 0], forward[:, 1], preferred_element_type=jnp.float32
    ) - jnp.einsum(pattern, backward[:, 1], forward[:, 0], preferred_element_type=jnp.float32)
    pair_re = pair_re.reshape(16, slices, -1)
    pair_im = pair_im.reshape(16, slices, -1)
    mat_re, mat_im = gamma_matrices(gamma_table)
    field_re, field_im = apply_gammas(mat_re, mat_im, pair_re, pair_im)
    fields = jnp.stack([field_re, field_im], 2).reshape(inserts * slices, 2, rows_x, rows_y, LZ)
    spectrum = transform(fields, source_site)
    local_re, local_im = project_sites(fields, source_site, momenta, rows_x, rows_y, L, LZ)
    listed_re, listed_im = lax.psum((local_re, local_im), ("sx", "sy"))
    listed_re = listed_re.reshape(inserts, slices, -1)
    listed_im = listed_im.reshape(inserts, slices, -1)
    corr_re = spectrum[:, 0].reshape(inserts, slices, spectrum.shape[2], -1)
    corr_im = spectrum[:, 1].reshape(inserts, slices, spectrum.shape[2], -1)
    return (jnp.stack([corr_re, corr_im], 2), jnp.stack([listed_re, listed_im], 0))


def solution(mesh):
    placed = (
        P(None, None, None, None, "sx", "sy"),
        P(None, None, None, None, "sx", "sy"),
        P(),
        P(),
        P(),
    )
    return jax.shard_map(
        body,
        mesh=mesh,
        in_specs=placed,
        out_specs=(P(None, None, None, "sx", "sy"), P()),
        check_vma=False,
    )
```

profile of v0, /device:TPU:1, one launch (start us, length us, event | category | flops | bytes accessed | tf_op | source)
XLA Modules:
  0.0 323.4 jit_solution(12954592644119887692)
XLA Ops:
  7.2 0.7 fusion.92
  7.9 2.1 reshape.371
  10.0 0.8 fusion.144
  10.9 4.5 %copy.82 = bf16[2,1,4,3,12,512]{4,2,3,5,0,1:T(4,128)(2,1)S(1)} copy(bf16[2,1,4,3,12,512]{5,4,3,2,1,0:T(8,128)(2,1)} %get-tuple-element.11) | data formatting | bytes 589824
  15.3 2.8 reshape.372
  18.1 2.1 fusion.145
  20.2 5.3 %copy.83 = bf16[2,1,4,3,12,512]{4,2,3,5,0,1:T(4,128)(2,1)} copy(bf16[2,1,4,3,12,512]{5,4,3,2,1,0:T(8,128)(2,1)} %get-tuple-element.13) | data formatting | bytes 589824
  25.4 3.8 %copy.80 = bf16[2,1,4,3,12,512]{4,2,3,5,0,1:T(4,128)(2,1)} copy(bf16[2,1,4,3,12,512]{5,4,3,2,1,0:T(8,128)(2,1)S(1)} %get-tuple-element.10) | data formatting | bytes 589824
  29.2 5.3 %copy.81 = bf16[2,1,4,3,12,512]{4,2,3,5,0,1:T(4,128)(2,1)} copy(bf16[2,1,4,3,12,512]{5,4,3,2,1,0:T(8,128)(2,1)} %get-tuple-element.12) | data formatting | bytes 589824
  34.5 5.6 %fusion.2 = f32[2,512,4,4,1]{3,2,4,1,0:T(4,128)S(1)} fusion(bf16[2,1,4,3,12,512]{4,2,3,5,0,1:T(4,128)(2,1)} %copy.83, bf16[2,1,4,3,12,512]{4,2,3,5,0,1:T(4,128)(2,1)S(1)} %copy.82), kind=kOutput, calls=%fused_computation.2 | convolution fusion | flops 1179648 | bytes 655360 | tf_op jit(solution)/shard_map/tscjn,tucjn->sutn/dot_general | solution.py:113
  40.2 5.0 %fusion = f32[2,512,4,4,1]{3,2,4,1,0:T(4,128)} fusion(bf16[2,1,4,3,12,512]{4,2,3,5,0,1:T(4,128)(2,1)S(1)} %copy-done.1, bf16[2,1,4,3,12,512]{4,2,3,5,0,1:T(4,128)(2,1)S(1)} %copy-done.2), kind=kOutput, calls=%fused_computation | convolution fusion | flops 1179648 | bytes 655360 | tf_op jit(solution)/shard_map/tscjn,tucjn->sutn/dot_general | solution.py:116
  45.2 3.7 %fusion.13 = f32[4,4,2,512]{0,1,3,2:T(4,128)} fusion(f32[2,512,4,4,1]{3,2,4,1,0:T(4,128)S(1)} %fusion.2, bf16[2,1,4,3,12,512]{4,2,3,5,0,1:T(4,128)(2,1)S(1)} %copy-done, bf16[2,1,4,3,12,512]{4,2,3,5,0,1:T(4,128)(2,1)S(1)} %copy-done.2), kind=kOutput, calls=%fused_computation.17 | convolution fusion | flops 1196032 | bytes 720896 | tf_op jit(solution)/shard_map/tscjn,tucjn->sutn/dot_general | solution.py:111
  48.8 2.1 copy.48
  51.0 7.5 %fusion.12 = f32[4,4,2,512]{0,1,3,2:T(4,128)} fusion(f32[2,512,4,4,1]{3,2,4,1,0:T(4,128)} %fusion, bf16[2,1,4,3,12,512]{4,2,3,5,0,1:T(4,128)(2,1)} %copy.81, bf16[2,1,4,3,12,512]{4,2,3,5,0,1:T(4,128)(2,1)S(1)} %copy.82), kind=kOutput, calls=%fused_computation.15 | convolution fusion | flops 1196032 | bytes 720896 | tf_op jit(solution)/shard_map/tscjn,tucjn->sutn/dot_general | solution.py:114
  58.5 1.9 copy.49
  60.5 0.7 fusion.146
  61.1 0.3 fusion.147
  61.4 0.3 fusion.148
  61.6 0.3 convolution_subtract_fusion.3
  61.9 0.1 squeeze.52
  62.0 1.3 and_select_fusion.1
  63.3 0.5 fusion.32
  63.8 0.5 fusion.30
  64.2 0.3 convolution_add_fusion.3
  64.5 0.1 squeeze.54
  64.6 0.5 fusion.25
  65.1 0.5 fusion.24
  65.5 0.7 pad_maximum_fusion
  66.3 0.6 iota_subtract_fusion
  67.0 0.7 add_subtract_fusion.1
  67.6 0.7 add_subtract_fusion
  68.6 0.1 fusion.45
  68.7 1.1 add_sine_fusion
  69.8 0.1 cos.29
  70.0 0.7 and_select_fusion.3
  70.7 0.2 fusion.149
  70.9 0.2 convolution_add_fusion.4
  71.1 107.5 %all-gather.2.cloned.1.call-done = f32[32,2,2,64,64]{4,0,3,2,1:T(8,128)} async-done(((f32[32,2,2,4,64]{4,0,3,2,1:T(8,128)}), f32[32,2,2,64,64]{4,0,3,2,1:T(8,128)}) %all-gather.2.cloned.1.call-update) | async-done | bytes 2097168 | tf_op jit(solution)/shard_map/all_gather | solution.py:54
  178.6 4.7 %dynamic-slice_bitcast_fusion = (f32[32,2,64,4]{3,0,2,1:T(8,128)S(1)}, f32[32,2,64,4]{3,0,2,1:T(8,128)}) fusion(f32[32,2,2,64,64]{4,0,3,2,1:T(8,128)} %all-gather.2.cloned.1.call-done, s32[]{:T(128)S(6)} %add.213, s32[]{:T(128)S(6)} %select_n.88), kind=kLoop, calls=%fused_computation.12 | loop fusion | bytes 262152 | tf_op jit(solution)/shard_map/squeeze | solution.py:56
  183.3 2.6 copy.54
  186.0 0.5 fusion.51
  186.4 0.5 fusion.53
  186.9 1.2 copy.55
  188.1 0.5 fusion.23
  188.5 0.5 fusion.22
  189.0 0.3 copy.58
  189.4 1.0 reshape.373
  190.4 13.0 %all-to-all-start = ((f32[32,1,1024]{2,1,0:T(1,128)}), f32[32,1,1024]{2,1,0:T(1,128)S(1)}, u32[]{:S(2)}, u32[]{:S(2)}) async-start(f32[32,1,1024]{2,1,0:T(1,128)} %reshape.373), calls=%async_computation | async-start | bytes 262144 | tf_op jit(solution)/shard_map/all_to_all | solution.py:58
  203.4 0.2 fusion.150
  203.6 0.2 convolution_subtract_fusion.4
  203.8 106.2 %all-reduce = (f32[1,16,2,32]{3,2,1,0:T(2,128)S(1)}, f32[1,16,2,32]{3,2,1,0:T(2,128)S(1)}) all-reduce(f32[1,16,2,32]{3,2,1,0:T(2,128)S(1)} %bitcast.184, f32[1,16,2,32]{3,2,1,0:T(2,128)S(1)} %bitcast.183), channel_id=1, replica_groups=mesh['sx'=32,'sy'=16] {'sx','sy'}, use_global_device_ids=true, to_apply=%region_1.2 | all-reduce | flops 2048 | bytes 16384 | tf_op jit(solution)/shard_map/psum | solution.py:124
  309.9 0.6 pad_maximum_fusion.3
  310.6 0.5 broadcast.522
  311.1 0.9 reduce
  312.0 0.3 reshape.374
  312.3 0.2 copy.59
  312.5 0.4 copy.60
  312.9 0.6 fusion.27
  313.5 0.6 fusion.26
  314.1 0.6 convolution_subtract_fusion.2
  314.9 0.1 stack_reshape_squeeze_stack.6
  315.0 0.6 convolution_add_fusion.2
  315.7 0.1 stack_reshape_squeeze_stack.7
  315.9 0.7 copy.65
  (29 shorter events, 0.8 us)
Async XLA Ops:
  7.2 171.4 %all-gather.2.cloned.1.call-start = ((), (), s32[]{:S(2)}) async-start(), calls=%async_computation.1 | async-start | bytes 4456448 | tf_op jit(solution)/shard_map/all_gather | solution.py:54
  34.5 5.6 %copy-start.1 = (bf16[2,1,4,3,12,512]{4,2,3,5,0,1:T(4,128)(2,1)S(1)}, bf16[2,1,4,3,12,512]{4,2,3,5,0,1:T(4,128)(2,1)}, u32[]{:S(2)}) copy-start(bf16[2,1,4,3,12,512]{4,2,3,5,0,1:T(4,128)(2,1)} %copy.83) | copy-start | bytes 884740
  34.5 5.6 %copy-start.2 = (bf16[2,1,4,3,12,512]{4,2,3,5,0,1:T(4,128)(2,1)S(1)}, bf16[2,1,4,3,12,512]{4,2,3,5,0,1:T(4,128)(2,1)}, u32[]{:S(2)}) copy-start(bf16[2,1,4,3,12,512]{4,2,3,5,0,1:T(4,128)(2,1)} %copy.80) | copy-start | bytes 884740
  40.2 5.0 %copy-start = (bf16[2,1,4,3,12,512]{4,2,3,5,0,1:T(4,128)(2,1)S(1)}, bf16[2,1,4,3,12,512]{4,2,3,5,0,1:T(4,128)(2,1)}, u32[]{:S(2)}) copy-start(bf16[2,1,4,3,12,512]{4,2,3,5,0,1:T(4,128)(2,1)} %copy.81) | copy-start | bytes 884740
  50.9 9.5 %copy-start.3 = (s32[3]{0:T(128)S(1)}, s32[3]{0:T(128)}, u32[]{:S(2)}) copy-start(s32[3]{0:T(128)} %param.8) | copy-start | bytes 40
  50.9 10.2 %slice-start = ((s32[16,4,2]{0,2,1:T(2,128)}), s32[16,4,1]{0,2,1:T(1,128)S(1)}, s32[]{:S(2)}) async-start(s32[16,4,2]{0,2,1:T(2,128)} %param.7), calls=%async_computation.2 | async-start | bytes 4096 | tf_op jit(solution)/shard_map/slice | solution.py:14
  58.5 9.8 %copy-start.4 = (s32[32,3]{0,1:T(4,128)S(1)}, s32[32,3]{0,1:T(4,128)}, u32[]{:S(2)}) copy-start(s32[32,3]{0,1:T(4,128)} %param.9) | copy-start | bytes 1156
  190.4 120.2 %all-to-all-start = ((f32[32,1,1024]{2,1,0:T(1,128)}), f32[32,1,1024]{2,1,0:T(1,128)S(1)}, u32[]{:S(2)}, u32[]{:S(2)}) async-start(f32[32,1,1024]{2,1,0:T(1,128)} %reshape.373), calls=%async_computation | async-start | bytes 262144 | tf_op jit(solution)/shard_map/all_to_all | solution.py:58
Sparse Core Ops, SparseCore 0:
  66.4 112.1 all-gather.1
where the time goes:
time: 325 us; the launch traced here: 323 us
  waiting for transfers between devices  108 us (33%)
  blocking collectives  106 us (33%)
  local copies, waits for them, and re-layouts  44.1 us (14%)
  matrix products  29.7 us (9%)
  between operations  14.4 us (4%)
  starting transfers between devices  13 us (4%)
  other arithmetic  8.45 us (3%)
    all_gather x1, waiting for transfers between devices, transform(): lax.all_gather(along_z, 'sy', axis=3, tiled=True)  107 us
    psum x1, blocking collectives, body(): listed_re, listed_im = lax.psum((local_re, local_im), ('sx', 'sy'))  106 us
    unnamed x19, local copies, waits for them, and re-layouts  20.8 us
    all_to_all x1, starting transfers between devices, transform(): lax.all_to_all(along_y, 'sx', split_axis=3, concat_axis=2, tiled=True)  13 us
    dot_general x1, matrix products, body(): jnp.einsum(pattern, backward[:, 0], forward[:, 1], preferred_element_type...  7.53 us
  transfers between devices with their start and end apart: 2, of which 1 were waited for; matrix products, arithmetic and copies ran while one was open for 2% of the time, Pallas kernels for 0%

commit v1 on v0

--- a/solution.py
+++ b/solution.py
@@ -7,6 +7,11 @@
 L = 64
 LZ = 64
 HIGHEST = lax.Precision.HIGHEST
+
+
+def by_each_axis(value, one, other):
+    inner = lax.psum(value, one)
+    return lax.psum(inner, other)
 
 
 def gamma_matrices(gamma_table):
@@ -121,7 +126,7 @@
     fields = jnp.stack([field_re, field_im], 2).reshape(inserts * slices, 2, rows_x, rows_y, LZ)
     spectrum = transform(fields, source_site)
     local_re, local_im = project_sites(fields, source_site, momenta, rows_x, rows_y, L, LZ)
-    listed_re, listed_im = lax.psum((local_re, local_im), ("sx", "sy"))
+    listed_re, listed_im = by_each_axis((local_re, local_im), "sx", "sy")
     listed_re = listed_re.reshape(inserts, slices, -1)
     listed_im = listed_im.reshape(inserts, slices, -1)
     corr_re = spectrum[:, 0].reshape(inserts, slices, spectrum.shape[2], -1)

time: 325 us -> 464 us (1.43)
  the two profiles are of different devices: /device:TPU:1 before, /device:TPU:0 now
where the time goes in v1:
time: 464 us; the launch traced here: 463 us
  blocking collectives  252 us (54%)
  waiting for transfers between devices  102 us (22%)
  local copies, waits for them, and re-layouts  44.1 us (10%)
  matrix products  29.8 us (6%)
  between operations  14.4 us (3%)
  starting transfers between devices  12.4 us (3%)
  other arithmetic  8.31 us (2%)
    psum x1, blocking collectives, by_each_axis(): inner = lax.psum(value, one)  175 us
    all_gather x1, waiting for transfers between devices, transform(): lax.all_gather(along_z, 'sy', axis=3, tiled=True)  102 us
    psum x1, blocking collectives, by_each_axis(): return lax.psum(inner, other)  77.8 us
    unnamed x19, local copies, waits for them, and re-layouts  20.8 us
    all_to_all x1, starting transfers between devices, transform(): lax.all_to_all(along_y, 'sx', split_axis=3, concat_axis=2, tiled=True)  12.3 us
  transfers between devices with their start and end apart: 2, of which 1 were waited for; matrix products, arithmetic and copies ran while one was open for 1% of the time, Pallas kernels for 0%

profile of v1, /device:TPU:0, one launch (start us, length us, event | category | flops | bytes accessed | tf_op | source)
XLA Modules:
  0.0 462.9 jit_solution(12240136589755531679)
XLA Ops:
  7.2 0.7 fusion.92
  7.9 2.1 reshape.371
  10.0 0.8 fusion.144
  10.8 4.5 copy.82
  15.3 2.8 reshape.372
  18.1 2.1 fusion.145
  20.2 5.3 %copy.83 = bf16[2,1,4,3,12,512]{4,2,3,5,0,1:T(4,128)(2,1)} copy(bf16[2,1,4,3,12,512]{5,4,3,2,1,0:T(8,128)(2,1)} %get-tuple-element.15) | data formatting | bytes 589824
  25.5 3.8 copy.80
  29.3 5.3 %copy.81 = bf16[2,1,4,3,12,512]{4,2,3,5,0,1:T(4,128)(2,1)} copy(bf16[2,1,4,3,12,512]{5,4,3,2,1,0:T(8,128)(2,1)} %get-tuple-element.14) | data formatting | bytes 589824
  34.6 5.6 %fusion.2 = f32[2,512,4,4,1]{3,2,4,1,0:T(4,128)S(1)} fusion(bf16[2,1,4,3,12,512]{4,2,3,5,0,1:T(4,128)(2,1)} %copy.83, bf16[2,1,4,3,12,512]{4,2,3,5,0,1:T(4,128)(2,1)S(1)} %copy.82), kind=kOutput, calls=%fused_computation.2 | convolution fusion | flops 1179648 | bytes 655360 | tf_op jit(solution)/shard_map/tscjn,tucjn->sutn/dot_general | solution.py:118
  40.2 5.0 %fusion = f32[2,512,4,4,1]{3,2,4,1,0:T(4,128)} fusion(bf16[2,1,4,3,12,512]{4,2,3,5,0,1:T(4,128)(2,1)S(1)} %copy-done.1, bf16[2,1,4,3,12,512]{4,2,3,5,0,1:T(4,128)(2,1)S(1)} %copy-done.2), kind=kOutput, calls=%fused_computation | convolution fusion | flops 1179648 | bytes 655360 | tf_op jit(solution)/shard_map/tscjn,tucjn->sutn/dot_general | solution.py:121
  45.2 3.7 fusion.13
  48.9 2.1 copy.48
  51.0 7.5 %fusion.12 = f32[4,4,2,512]{0,1,3,2:T(4,128)} fusion(f32[2,512,4,4,1]{3,2,4,1,0:T(4,128)} %fusion, bf16[2,1,4,3,12,512]{4,2,3,5,0,1:T(4,128)(2,1)} %copy.81, bf16[2,1,4,3,12,512]{4,2,3,5,0,1:T(4,128)(2,1)S(1)} %copy.82), kind=kOutput, calls=%fused_computation.15 | convolution fusion | flops 1196032 | bytes 720896 | tf_op jit(solution)/shard_map/tscjn,tucjn->sutn/dot_general | solution.py:119
  58.6 1.9 copy.49
  60.5 0.6 fusion.146
  61.1 0.3 fusion.147
  61.4 0.3 fusion.148
  61.6 0.3 convolution_subtract_fusion.3
  61.9 0.1 squeeze.52
  62.0 1.2 and_select_fusion.1
  63.2 0.5 fusion.32
  63.7 0.5 fusion.30
  64.2 0.3 convolution_add_fusion.3
  64.4 0.1 squeeze.54
  64.5 0.5 fusion.25
  65.0 0.5 fusion.24
  65.5 0.7 pad_maximum_fusion
  66.3 0.6 iota_subtract_fusion
  66.8 0.7 add_subtract_fusion.1
  67.5 0.7 add_subtract_fusion
  68.4 0.1 fusion.45
  68.6 1.1 add_sine_fusion
  69.9 0.7 and_select_fusion.3
  70.6 0.2 fusion.149
  70.8 0.2 convolution_add_fusion.4
  71.0 101.6 %all-gather.2.cloned.1.call-done = f32[32,2,2,64,64]{4,0,3,2,1:T(8,128)} async-done(((f32[32,2,2,4,64]{4,0,3,2,1:T(8,128)}), f32[32,2,2,64,64]{4,0,3,2,1:T(8,128)}) %all-gather.2.cloned.1.call-update) | async-done | bytes 2097168 | tf_op jit(solution)/shard_map/all_gather | solution.py:59
  172.6 4.7 %dynamic-slice_bitcast_fusion = (f32[32,2,64,4]{3,0,2,1:T(8,128)S(1)}, f32[32,2,64,4]{3,0,2,1:T(8,128)}) fusion(f32[32,2,2,64,64]{4,0,3,2,1:T(8,128)} %all-gather.2.cloned.1.call-done, s32[]{:T(128)S(6)} %add.217, s32[]{:T(128)S(6)} %select_n.88), kind=kLoop, calls=%fused_computation.12 | loop fusion | bytes 262152 | tf_op jit(solution)/shard_map/squeeze | solution.py:61
  177.3 2.6 copy.54
  179.9 0.5 fusion.51
  180.4 0.5 fusion.53
  180.8 1.2 copy.55
  182.0 0.5 fusion.23
  182.5 0.5 fusion.22
  183.0 0.3 copy.58
  183.3 1.0 reshape.373
  184.3 12.3 %all-to-all-start = ((f32[32,1,1024]{2,1,0:T(1,128)}), f32[32,1,1024]{2,1,0:T(1,128)S(1)}, u32[]{:S(2)}, u32[]{:S(2)}) async-start(f32[32,1,1024]{2,1,0:T(1,128)} %reshape.373), calls=%async_computation | async-start | bytes 262144 | tf_op jit(solution)/shard_map/all_to_all | solution.py:63
  196.6 0.2 fusion.150
  196.8 0.2 convolution_subtract_fusion.4
  197.0 174.6 %all-reduce = (f32[32,32]{1,0:T(8,128)S(1)}, f32[32,32]{1,0:T(8,128)S(1)}) all-reduce(f32[32,32]{1,0:T(8,128)S(1)} %convolution_subtract_fusion.4, f32[32,32]{1,0:T(8,128)S(1)} %convolution_add_fusion.4), channel_id=1, replica_groups=mesh['sx'=32,'sy'=16] {'sx'}, use_global_device_ids=true, to_apply=%region_2.3 | all-reduce | flops 2048 | bytes 16384 | tf_op jit(solution)/shard_map/psum | solution.py:13
  371.6 77.8 %all-reduce.1 = (f32[1,16,2,32]{3,2,1,0:T(2,128)S(1)}, f32[1,16,2,32]{3,2,1,0:T(2,128)S(1)}) all-reduce(f32[1,16,2,32]{3,2,1,0:T(2,128)S(1)} %bitcast.183, f32[1,16,2,32]{3,2,1,0:T(2,128)S(1)} %bitcast.184), channel_id=1, replica_groups=mesh['sx'=32,'sy'=16] {'sy'}, use_global_device_ids=true, to_apply=%region_3.4 | all-reduce | flops 2048 | bytes 16384 | tf_op jit(solution)/shard_map/psum | solution.py:14
  449.4 0.6 pad_maximum_fusion.3
  450.1 0.5 broadcast.522
  450.6 0.9 reduce
  451.5 0.3 reshape.374
  451.8 0.2 copy.59
  452.0 0.4 copy.60
  452.4 0.6 fusion.27
  453.0 0.6 fusion.26
  453.7 0.6 convolution_subtract_fusion.2
  454.4 0.1 stack_reshape_squeeze_stack.6
  454.5 0.6 convolution_add_fusion.2
  455.2 0.1 stack_reshape_squeeze_stack.7
  455.4 0.7 copy.65
  (30 shorter events, 0.9 us)
Async XLA Ops:
  7.2 165.4 %all-gather.2.cloned.1.call-start = ((), (), s32[]{:S(2)}) async-start(), calls=%async_computation.1 | async-start | bytes 4456448 | tf_op jit(solution)/shard_map/all_gather | solution.py:59
  34.5 5.6 %copy-start.1 = (bf16[2,1,4,3,12,512]{4,2,3,5,0,1:T(4,128)(2,1)S(1)}, bf16[2,1,4,3,12,512]{4,2,3,5,0,1:T(4,128)(2,1)}, u32[]{:S(2)}) copy-start(bf16[2,1,4,3,12,512]{4,2,3,5,0,1:T(4,128)(2,1)} %copy.83) | copy-start | bytes 884740
  34.6 5.6 %copy-start.2 = (bf16[2,1,4,3,12,512]{4,2,3,5,0,1:T(4,128)(2,1)S(1)}, bf16[2,1,4,3,12,512]{4,2,3,5,0,1:T(4,128)(2,1)}, u32[]{:S(2)}) copy-start(bf16[2,1,4,3,12,512]{4,2,3,5,0,1:T(4,128)(2,1)} %copy.80) | copy-start | bytes 884740
  40.2 5.0 %copy-start = (bf16[2,1,4,3,12,512]{4,2,3,5,0,1:T(4,128)(2,1)S(1)}, bf16[2,1,4,3,12,512]{4,2,3,5,0,1:T(4,128)(2,1)}, u32[]{:S(2)}) copy-start(bf16[2,1,4,3,12,512]{4,2,3,5,0,1:T(4,128)(2,1)} %copy.81) | copy-start | bytes 884740
  51.0 9.5 %copy-start.3 = (s32[3]{0:T(128)S(1)}, s32[3]{0:T(128)}, u32[]{:S(2)}) copy-start(s32[3]{0:T(128)} %param.8) | copy-start | bytes 40
  51.0 10.1 %slice-start = ((s32[16,4,2]{0,2,1:T(2,128)}), s32[16,4,1]{0,2,1:T(1,128)S(1)}, s32[]{:S(2)}) async-start(s32[16,4,2]{0,2,1:T(2,128)} %param.7), calls=%async_computation.2 | async-start | bytes 4096 | tf_op jit(solution)/shard_map/slice | solution.py:19
  58.6 9.6 %copy-start.4 = (s32[32,3]{0,1:T(4,128)S(1)}, s32[32,3]{0,1:T(4,128)}, u32[]{:S(2)}) copy-start(s32[32,3]{0,1:T(4,128)} %param.9) | copy-start | bytes 1156
  184.3 265.8 %all-to-all-start = ((f32[32,1,1024]{2,1,0:T(1,128)}), f32[32,1,1024]{2,1,0:T(1,128)S(1)}, u32[]{:S(2)}, u32[]{:S(2)}) async-start(f32[32,1,1024]{2,1,0:T(1,128)} %reshape.373), calls=%async_computation | async-start | bytes 262144 | tf_op jit(solution)/shard_map/all_to_all | solution.py:63
Sparse Core Ops, SparseCore 0:
  66.3 106.1 all-gather.1
